TPU v7x, 256 devices: a whole 4x4x8 slice. The times are simulated.
256 devices in a mesh: seq: 64 (over y, z, core), ch: 4 (over x).
Axes of the slice: x: 4, y: 4, z: 8, core: 2. Of those that a mesh axis runs over, the one named last changes fastest.
Arguments:
- features: bfloat16 [32768, 1024], P('seq', 'ch'), may hold values from -6 to 6
- w_in: bfloat16 [1024, 3, 1024], P(None, None, 'ch'), may hold values from -0.1875 to 0.1875
- bias_skip: float32 [1024], P('ch'), may hold values from -3 to 3
- filters: float32 [32768, 1024], P('seq', 'ch')
- w_out: bfloat16 [1024, 1024], P(None, 'ch'), may hold values from -0.1875 to 0.1875
- w_emb: bfloat16 [1024, 128], P('ch'), may hold values from -0.1875 to 0.1875
- page_lengths: int32 [512], replicated, may hold values from 1 to 256, 32768 in all
- page_owner: int32 [512], replicated, may hold values from 0 to 63
Outputs:
- index_rows: bfloat16 [32768, 128], P('seq')
Inputs may be any that keep to these rules, and one draw needn't show every extreme that they name: page_lengths sum to 32768, and the longest page has exactly 256 patches.
All inputs are finite; a program needn't handle non-finite values.
Results may differ from a plain program's by a relative error of at most 0.0057.
Values may be sent and summed in bfloat16 or wider, within the bound.
A program may use at most 64 MiB of HBM per device.

v0:
```python
import math

import jax
import jax.numpy as jnp
from jax import lax
from jax.sharding import PartitionSpec as P


def angle_table(first_index, second_index, period):
    product = first_index[:, None] * second_index[None, :] % period
    return product.astype(jnp.float32) * (2.0 * math.pi / period)


def apply_table(table, values):
    return jnp.einsum("ki,qic->qkc", table, values, precision=lax.Precision.HIGHEST)


def long_convolution(signal, filters, seq_count, seq_rank):
    rows_dev, chan_dev = signal.shape
    group_rows = rows_dev // seq_count
    block_count = 2 * seq_count
    fft_length = block_count * rows_dev
    block_index = jnp.arange(block_count, dtype=jnp.int32)
    source_index = jnp.arange(seq_count, dtype=jnp.int32)
    outer_angle = angle_table(block_index, source_index, block_count)
    outer_cos = jnp.cos(outer_angle)
    outer_sin = jnp.sin(outer_angle)
    local_rows = seq_rank * group_rows + jnp.arange(group_rows, dtype=jnp.int32)
    twist_angle = angle_table(block_index, local_rows, fft_length)
    twist_cos = jnp.cos(twist_angle)[:, :, None]
    twist_sin = jnp.sin(twist_angle)[:, :, None]
    inner_index = jnp.arange(rows_dev, dtype=jnp.int32)
    inner_angle = angle_table(inner_index, inner_index, rows_dev)
    inner_cos = jnp.cos(inner_angle)
    inner_sin = jnp.sin(inner_angle)
    signal_blocks, filter_blocks = (
        lax.all_to_all(
            signal.reshape(seq_count, group_rows, chan_dev),
            "seq",
            split_axis=0,
            concat_axis=0,
            tiled=True,
        ),
        lax.all_to_all(
            filters.reshape(seq_count, group_rows, chan_dev),
            "seq",
            split_axis=0,
            concat_axis=0,
            tiled=True,
        ),
    )

    def outer_forward(blocks):
        real_part = jnp.einsum("kj,jic->kic", outer_cos, blocks, precision=lax.Precision.HIGHEST)
        imag_part = -jnp.einsum("kj,jic->kic", outer_sin, blocks, precision=lax.Precision.HIGHEST)
        return jnp.stack(
            [
                real_part * twist_cos + imag_part * twist_sin,
                imag_part * twist_cos - real_part * twist_sin,
            ]
        )

    signal_spec, filter_spec = (
        lax.all_to_all(
            outer_forward(signal_blocks), "seq", split_axis=1, concat_axis=2, tiled=True
        ),
        lax.all_to_all(
            outer_forward(filter_blocks), "seq", split_axis=1, concat_axis=2, tiled=True
        ),
    )

    def inner_forward(spectrum):
        real_in = spectrum[0]
        imag_in = spectrum[1]
        return (
            apply_table(inner_cos, real_in) + apply_table(inner_sin, imag_in),
            apply_table(inner_cos, imag_in) - apply_table(inner_sin, real_in),
        )

    signal_real, signal_imag = inner_forward(signal_spec)
    filter_real, filter_imag = inner_forward(filter_spec)
    product_real = signal_real * filter_real - signal_imag * filter_imag
    product_imag = signal_real * filter_imag + signal_imag * filter_real
    back_real = apply_table(inner_cos, product_real) - apply_table(inner_sin, product_imag)
    back_imag = apply_table(inner_cos, product_imag) + apply_table(inner_sin, product_real)
    returned = lax.all_to_all(
        jnp.stack([back_real, back_imag]), "seq", split_axis=2, concat_axis=1, tiled=True
    )
    turned_real = returned[0] * twist_cos - returned[1] * twist_sin
    turned_imag = returned[0] * twist_sin + returned[1] * twist_cos
    result = (
        jnp.einsum("kj,kic->jic", outer_cos, turned_real, precision=lax.Precision.HIGHEST)
        - jnp.einsum("kj,kic->jic", outer_sin, turned_imag, precision=lax.Precision.HIGHEST)
    ) / fft_length
    back_tokens = lax.all_to_all(result, "seq", split_axis=0, concat_axis=1, tiled=True)
    return back_tokens.reshape(rows_dev, chan_dev)


def source_tokens(page_lengths, page_owner, output_rows):
    page_index = jnp.arange(page_lengths.shape[0], dtype=jnp.int32)
    before = (page_owner[None, :] < page_owner[:, None]) | (
        page_owner[None, :] == page_owner[:, None]
    ) & (page_index[None, :] < page_index[:, None])
    placed_start = jnp.sum(jnp.where(before, page_lengths[None, :], 0), axis=1)
    page_start = jnp.cumsum(page_lengths) - page_lengths
    inside = (output_rows[:, None] >= placed_start[None, :]) & (
        output_rows[:, None] < (placed_start + page_lengths)[None, :]
    )
    offsets = page_start[None, :] + output_rows[:, None] - placed_start[None, :]
    return jnp.sum(jnp.where(inside, offsets, 0), axis=1)


def body(features, w_in, bias_skip, filters, w_out, w_emb, page_lengths, page_owner):
    rows_dev, chan_dev = features.shape
    seq_count = lax.axis_size("seq")
    seq_rank = lax.axis_index("seq")
    flat_in = w_in.reshape(w_in.shape[0], -1)
    weight_rows = flat_in
    projected = jnp.dot(
        lax.all_gather(features, "ch", axis=1, tiled=True),
        weight_rows,
        preferred_element_type=jnp.float32,
    )
    projected = projected.reshape(rows_dev, 3, chan_dev)
    gate_branch = projected[:, 0]
    signal = projected[:, 1] * projected[:, 2]
    convolved = long_convolution(signal, filters, seq_count, seq_rank)
    mixed = ((convolved + bias_skip[None, :] * signal) * gate_branch).astype(jnp.bfloat16)
    weight_rows = w_out
    summed = jnp.dot(
        lax.all_gather(mixed, "ch", axis=1, tiled=True),
        weight_rows,
        preferred_element_type=jnp.float32,
    )
    layer_out = (summed + features.astype(jnp.float32)).astype(jnp.bfloat16)
    output_rows = seq_rank * rows_dev + jnp.arange(rows_dev, dtype=jnp.int32)
    source = source_tokens(page_lengths, page_owner, output_rows)
    embedded = lax.psum(jnp.dot(layer_out, w_emb, preferred_element_type=jnp.float32), "ch").astype(
        jnp.bfloat16
    )
    shard_part = lax.all_gather(embedded, "seq", axis=0, tiled=True)
    count_rows = shard_part.shape[0]
    inside = (source >= 0) & (source < count_rows)
    taken = jnp.take(shard_part, jnp.clip(source, 0, count_rows - 1), axis=0)
    return jnp.where(inside[:, None], taken, jnp.zeros_like(embedded))


def solution(mesh):
    return jax.shard_map(
        body,
        mesh=mesh,
        in_specs=(
            P("seq", "ch"),
            P(None, None, "ch"),
            P("ch"),
            P("seq", "ch"),
            P(None, "ch"),
            P("ch", None),
            P(),
            P(),
        ),
        out_specs=P("seq", None),
        check_vma=False,
    )
```

profile of v0, /device:TPU:1, one launch (start us, length us, event | category | flops | bytes accessed | tf_op | source)
XLA Modules:
  0.0 488.9 jit_solution(5704225290694879429)
XLA Ops:
  7.3 13.2 %all-to-all-start.2 = ((f32[64,8,256]{2,1,0:T(8,128)}), f32[64,8,256]{2,1,0:T(8,128)S(1)}, u32[]{:S(2)}, u32[]{:S(2)}) async-start(f32[64,8,256]{2,1,0:T(8,128)} %bitcast.145), calls=%async_computation.2 | async-start | bytes 1048576 | tf_op jit(solution)/shard_map/all_to_all | solution.py:44
  20.4 1.7 copy.53
  22.1 17.4 %all-gather.4.cloned.1.call-done = bf16[512,1024]{1,0:T(8,128)(2,1)} async-done(((bf16[512,256]{1,0:T(8,128)(2,1)}), bf16[512,1024]{1,0:T(8,128)(2,1)}) %all-gather.4.cloned.1.call-update) | async-done | bytes 1048592 | tf_op jit(solution)/shard_map/all_gather | solution.py:120
  39.6 2.2 fusion
  41.8 1.2 copy-done.2
  43.0 0.9 fusion.89
  43.9 12.0 %all-to-all-start = ((f32[64,8,256]{2,1,0:T(8,128)}), f32[64,8,256]{2,1,0:T(8,128)S(1)}, u32[]{:S(2)}, u32[]{:S(2)}) async-start(f32[64,8,256]{2,1,0:T(8,128)} %fusion.89), calls=%async_computation | async-start | bytes 1048576 | tf_op jit(solution)/shard_map/all_to_all | solution.py:37
  56.0 1.2 convolution_negate_fusion
  57.2 2.2 fusion.84
  59.4 13.8 %all-to-all-done = f32[64,8,256]{2,1,0:T(8,128)S(1)} async-done(((f32[64,8,256]{2,1,0:T(8,128)}), f32[64,8,256]{2,1,0:T(8,128)S(1)}, u32[]{:S(2)}, u32[]{:S(2)}) %all-to-all-start) | async-done | bytes 524320 | tf_op jit(solution)/shard_map/all_to_all | solution.py:37
  73.2 1.2 convolution_negate_fusion.1
  74.4 2.9 add_bitcast_fusion
  77.5 2.5 copy.64
  80.0 6.8 %all-to-all-start.3 = ((f32[2,128,8,256]{3,2,0,1:T(8,128)}), f32[2,128,8,256]{3,2,0,1:T(8,128)S(1)}, u32[]{:S(2)}, u32[]{:S(2)}) async-start(f32[2,128,8,256]{3,2,0,1:T(8,128)} %copy.64), calls=%async_computation.3 | async-start | bytes 4194304 | tf_op jit(solution)/shard_map/all_to_all | solution.py:67
  86.8 1.7 pad_maximum_fusion
  88.5 2.6 copy.56
  91.0 46.9 %all-to-all-done.3 = f32[2,128,8,256]{3,2,0,1:T(8,128)S(1)} async-done(((f32[2,128,8,256]{3,2,0,1:T(8,128)}), f32[2,128,8,256]{3,2,0,1:T(8,128)S(1)}, u32[]{:S(2)}, u32[]{:S(2)}) %all-to-all-start.3) | async-done | bytes 2097184 | tf_op jit(solution)/shard_map/all_to_all | solution.py:67
  138.0 1.3 copy-done.1
  139.3 5.8 %all-to-all-start.1 = ((f32[2,128,8,256]{3,2,0,1:T(8,128)}), f32[2,128,8,256]{3,2,0,1:T(8,128)S(1)}, u32[]{:S(2)}, u32[]{:S(2)}) async-start(f32[2,128,8,256]{3,2,0,1:T(8,128)} %copy.56), calls=%async_computation.1 | async-start | bytes 4194304 | tf_op jit(solution)/shard_map/all_to_all | solution.py:64
  145.1 1.7 copy.65
  147.0 7.2 %fusion.16 = f32[2,256,512]{2,1,0:T(8,128)S(1)} fusion(f32[1,2,64,8,256]{4,3,1,2,0:T(8,128)S(1)} %get-tuple-element.13), kind=kOutput, calls=%fused_computation.34 | convolution fusion | flops 1614282752 | bytes 2097152 | tf_op jit(solution)/shard_map/ki,qic->qkc/dot_general | solution.py:15
  154.2 7.4 %fusion.20 = f32[2,256,512]{2,1,0:T(8,128)S(1)} fusion(f32[1,2,64,8,256]{4,3,1,2,0:T(8,128)S(1)} %get-tuple-element.14), kind=kOutput, calls=%fused_computation.38 | convolution fusion | flops 1614282752 | bytes 2097152 | tf_op jit(solution)/shard_map/ki,qic->qkc/dot_general | solution.py:15
  161.6 8.1 %convolution_subtract_fusion.1 = f32[2,256,512]{2,1,0:T(8,128)} fusion(f32[2,256,512]{2,1,0:T(8,128)S(1)} %fusion.16, f32[1,2,64,8,256]{4,3,1,2,0:T(8,128)S(1)} %get-tuple-element.14), kind=kOutput, calls=%fused_computation.16 | convolution fusion | flops 1614544896 | bytes 3145728 | tf_op jit(solution)/shard_map/ki,qic->qkc/dot_general | solution.py:15
  169.7 8.3 %convolution_add_fusion.1 = f32[2,256,512]{2,1,0:T(8,128)} fusion(f32[2,256,512]{2,1,0:T(8,128)S(1)} %fusion.20, f32[1,2,64,8,256]{4,3,1,2,0:T(8,128)S(1)} %get-tuple-element.13), kind=kOutput, calls=%fused_computation.18 | convolution fusion | flops 1614544896 | bytes 3145728 | tf_op jit(solution)/shard_map/ki,qic->qkc/dot_general | solution.py:15
  178.0 18.3 %all-to-all-done.1 = f32[2,128,8,256]{3,2,0,1:T(8,128)S(1)} async-done(((f32[2,128,8,256]{3,2,0,1:T(8,128)}), f32[2,128,8,256]{3,2,0,1:T(8,128)S(1)}, u32[]{:S(2)}, u32[]{:S(2)}) %all-to-all-start.1) | async-done | bytes 2097184 | tf_op jit(solution)/shard_map/all_to_all | solution.py:64
  196.6 7.2 %fusion.36 = f32[2,256,512]{2,1,0:T(8,128)S(1)} fusion(f32[1,2,64,8,256]{4,3,1,2,0:T(8,128)S(1)} %get-tuple-element.15), kind=kOutput, calls=%fused_computation.54 | convolution fusion | flops 1614282752 | bytes 2097152 | tf_op jit(solution)/shard_map/ki,qic->qkc/dot_general | solution.py:15
  203.8 7.6 %fusion.28 = f32[2,256,512]{2,1,0:T(8,128)S(1)} fusion(f32[1,2,64,8,256]{4,3,1,2,0:T(8,128)S(1)} %get-tuple-element.16), kind=kOutput, calls=%fused_computation.46 | convolution fusion | flops 1614282752 | bytes 2097152 | tf_op jit(solution)/shard_map/ki,qic->qkc/dot_general | solution.py:15
  211.4 7.2 %convolution_add_fusion.2 = f32[2,256,512]{2,1,0:T(8,128)S(1)} fusion(f32[2,256,512]{2,1,0:T(8,128)S(1)} %fusion.36, f32[1,2,64,8,256]{4,3,1,2,0:T(8,128)S(1)} %get-tuple-element.16), kind=kOutput, calls=%fused_computation.19 | convolution fusion | flops 1614544896 | bytes 3145728 | tf_op jit(solution)/shard_map/ki,qic->qkc/dot_general | solution.py:15
  218.6 7.6 %multiply_subtract_fusion = (f32[2,256,512]{2,1,0:T(8,128)S(1)}, f32[2,256,512]{2,1,0:T(8,128)S(1)}) fusion(f32[2,256,512]{2,1,0:T(8,128)S(1)} %copy-done.5, f32[2,256,512]{2,1,0:T(8,128)S(1)} %convolution_add_fusion.2, f32[2,256,512]{2,1,0:T(8,128)S(1)} %copy-done.6, f32[2,256,512]{2,1,0:T(8,128)S(1)} %fusion.28, ...), kind=kOutput, calls=%fused_computation.67 | convolution fusion | flops 1616117760 | bytes 7340032 | tf_op jit(solution)/shard_map/ki,qic->qkc/dot_general | solution.py:15
  226.2 6.3 %fusion.14 = f32[2,256,512]{2,1,0:T(8,128)S(1)} fusion(f32[2,256,512]{2,1,0:T(8,128)S(1)} %get-tuple-element.5), kind=kOutput, calls=%fused_computation.32 | convolution fusion | flops 1614282752 | bytes 2097152 | tf_op jit(solution)/shard_map/ki,qic->qkc/dot_general | solution.py:15
  232.6 6.5 %fusion.10 = f32[2,256,512]{2,1,0:T(8,128)S(1)} fusion(f32[2,256,512]{2,1,0:T(8,128)S(1)} %get-tuple-element.6), kind=kOutput, calls=%fused_computation.28 | convolution fusion | flops 1614282752 | bytes 2097152 | tf_op jit(solution)/shard_map/ki,qic->qkc/dot_general | solution.py:15
  239.1 6.3 %fusion.3 = f32[1,2,512,256]{2,3,1,0:T(8,128)S(1)} fusion(f32[2,256,512]{2,1,0:T(8,128)S(1)} %fusion.14, f32[2,256,512]{2,1,0:T(8,128)S(1)} %get-tuple-element.6), kind=kOutput, calls=%fused_computation.15 | convolution fusion | flops 1614544896 | bytes 3145728 | tf_op jit(solution)/shard_map/ki,qic->qkc/dot_general | solution.py:15
  245.5 6.3 %fusion.2 = f32[1,2,512,256]{2,3,1,0:T(8,128)S(1)} fusion(f32[2,256,512]{2,1,0:T(8,128)S(1)} %fusion.10, f32[2,256,512]{2,1,0:T(8,128)S(1)} %get-tuple-element.5), kind=kOutput, calls=%fused_computation.13 | convolution fusion | flops 1614544896 | bytes 3145728 | tf_op jit(solution)/shard_map/ki,qic->qkc/dot_general | solution.py:15
  252.0 2.5 copy.74
  254.5 57.4 %all_to_all.64 = f32[2,2,512,256]{3,1,0,2:T(2,128)S(1)} all-to-all(f32[2,2,512,256]{3,1,0,2:T(2,128)} %copy.74), channel_id=1, replica_groups=mesh['seq'=64,'ch'=4] {'seq'}, dimensions={2} | all-to-all | bytes 4194304 | tf_op jit(solution)/shard_map/all_to_all | solution.py:86
  312.3 1.1 fusion.190
  314.9 3.0 copy.77
  317.9 1.9 squeeze.30
  319.9 1.0 fusion.44
  320.9 1.0 fusion.4
  322.2 23.0 %all_to_all.65 = f32[64,8,256]{2,1,0:T(8,128)S(1)} all-to-all(f32[64,8,256]{2,1,0:T(8,128)S(1)} %copy.78), channel_id=1, replica_groups=mesh['seq'=64,'ch'=4] {'seq'}, dimensions={0} | all-to-all | bytes 1048576 | tf_op jit(solution)/shard_map/all_to_all | solution.py:95
  345.2 0.9 fusion.62
  346.1 23.0 %all-gather.6.cloned.1.call-done = bf16[512,1024]{1,0:T(8,128)(2,1)} async-done(((bf16[512,256]{1,0:T(8,128)(2,1)}), bf16[512,1024]{1,0:T(8,128)(2,1)}) %all-gather.6.cloned.1.call-update) | async-done | bytes 1048592 | tf_op jit(solution)/shard_map/all_gather | solution.py:131
  369.1 1.8 fusion.6
  371.0 15.8 %all-reduce.1 = bf16[512,128]{1,0:T(8,128)(2,1)} all-reduce(f32[512,128]{1,0:T(8,128)S(1)} %fusion.6), channel_id=1, replica_groups=mesh['seq'=64,'ch'=4] {'ch'}, use_global_device_ids=true, to_apply=%region_4.5 | all-reduce | flops 65536 | bytes 393216 | tf_op jit(solution)/shard_map/psum | solution.py:138
  388.2 87.3 %all-gather.8.cloned.1.call-done = bf16[32768,128]{1,0:T(8,128)(2,1)} async-done(((bf16[512,128]{1,0:T(8,128)(2,1)}), bf16[32768,128]{1,0:T(8,128)(2,1)}) %all-gather.8.cloned.1.call-update) | async-done | bytes 8388624 | tf_op jit(solution)/shard_map/all_gather | solution.py:141
  475.5 5.5 %gather_fusion = bf16[512,128]{1,0:T(8,128)(2,1)S(1)} fusion(bf16[32768,128]{1,0:T(8,128)(2,1)} %all-gather.8.cloned.1.call-done, s32[1024]{0:T(1024)S(1)} %pad_clamp_fusion), kind=kCustom, calls=%fused_computation | custom fusion | bytes 264192 | tf_op jit(solution)/shard_map/jit(_take)/gather | solution.py:144
  481.0 0.9 select_select_fusion
  (51 shorter events, 5.5 us)
Async XLA Ops:
  6.5 362.6 %copy-start = (bf16[1024,256]{1,0:T(8,128)(2,1)S(1)}, bf16[1024,256]{1,0:T(8,128)(2,1)}, u32[]{:S(2)}) copy-start(bf16[1024,256]{1,0:T(8,128)(2,1)} %param.12) | copy-start | bytes 1572868
  6.5 33.0 %all-gather.4.cloned.1.call-start = ((), (), s32[]{:S(2)}) async-start(), calls=%async_computation.6 | async-start | bytes 1310720 | tf_op jit(solution)/shard_map/all_gather | solution.py:120
  7.3 36.6 %all-to-all-start.2 = ((f32[64,8,256]{2,1,0:T(8,128)}), f32[64,8,256]{2,1,0:T(8,128)S(1)}, u32[]{:S(2)}, u32[]{:S(2)}) async-start(f32[64,8,256]{2,1,0:T(8,128)} %bitcast.145), calls=%async_computation.2 | async-start | bytes 1048576 | tf_op jit(solution)/shard_map/all_to_all | solution.py:44
  41.8 1.2 copy-start.2
  43.9 29.3 %all-to-all-start = ((f32[64,8,256]{2,1,0:T(8,128)}), f32[64,8,256]{2,1,0:T(8,128)S(1)}, u32[]{:S(2)}, u32[]{:S(2)}) async-start(f32[64,8,256]{2,1,0:T(8,128)} %fusion.89), calls=%async_computation | async-start | bytes 1048576 | tf_op jit(solution)/shard_map/all_to_all | solution.py:37
  73.2 1.2 copy-start.4
  80.0 57.9 %all-to-all-start.3 = ((f32[2,128,8,256]{3,2,0,1:T(8,128)}), f32[2,128,8,256]{3,2,0,1:T(8,128)S(1)}, u32[]{:S(2)}, u32[]{:S(2)}) async-start(f32[2,128,8,256]{3,2,0,1:T(8,128)} %copy.64), calls=%async_computation.3 | async-start | bytes 4194304 | tf_op jit(solution)/shard_map/all_to_all | solution.py:67
  138.0 1.3 copy-start.1
  139.3 57.0 %all-to-all-start.1 = ((f32[2,128,8,256]{3,2,0,1:T(8,128)}), f32[2,128,8,256]{3,2,0,1:T(8,128)S(1)}, u32[]{:S(2)}, u32[]{:S(2)}) async-start(f32[2,128,8,256]{3,2,0,1:T(8,128)} %copy.56), calls=%async_computation.1 | async-start | bytes 4194304 | tf_op jit(solution)/shard_map/all_to_all | solution.py:64
  145.0 224.1 %all-gather.6.cloned.1.call-start = ((), (), s32[]{:S(2)}) async-start(), calls=%async_computation.7 | async-start | bytes 1310720 | tf_op jit(solution)/shard_map/all_gather | solution.py:131
  211.4 7.2 %copy-start.5 = (f32[2,256,512]{2,1,0:T(8,128)S(1)}, f32[2,256,512]{2,1,0:T(8,128)}, u32[]{:S(2)}) copy-start(f32[2,256,512]{2,1,0:T(8,128)} %convolution_subtract_fusion.1) | copy-start | bytes 3145732
  211.4 7.2 %copy-start.6 = (f32[2,256,512]{2,1,0:T(8,128)S(1)}, f32[2,256,512]{2,1,0:T(8,128)}, u32[]{:S(2)}) copy-start(f32[2,256,512]{2,1,0:T(8,128)} %convolution_add_fusion.1) | copy-start | bytes 3145732
  320.9 24.3 %copy-start.3 = (f32[512,3,256]{2,0,1:T(8,128)S(1)}, f32[512,3,256]{2,0,1:T(8,128)}, u32[]{:S(2)}) copy-start(f32[512,3,256]{2,0,1:T(8,128)} %copy-done.2) | copy-start | bytes 4718596
  320.9 24.3 %copy-start.10 = (f32[256]{0:T(256)S(1)}, f32[256]{0:T(256)}, u32[]{:S(2)}) copy-start(f32[256]{0:T(256)} %param.10) | copy-start | bytes 3076
  322.2 46.9 %copy-start.7 = (bf16[512,256]{1,0:T(8,128)(2,1)S(1)}, bf16[512,256]{1,0:T(8,128)(2,1)}, u32[]{:S(2)}) copy-start(bf16[512,256]{1,0:T(8,128)(2,1)} %param.8) | copy-start | bytes 786436
  322.2 46.9 %copy-start.11 = (bf16[256,128]{1,0:T(8,128)(2,1)S(1)}, bf16[256,128]{1,0:T(8,128)(2,1)}, u32[]{:S(2)}) copy-start(bf16[256,128]{1,0:T(8,128)(2,1)} %param.13) | copy-start | bytes 196612
  346.0 40.8 %copy-start.8 = (s32[512]{0:T(512)S(1)}, s32[512]{0:T(512)}, u32[]{:S(2)}) copy-start(s32[512]{0:T(512)} %param.14) | copy-start | bytes 6148
  346.0 41.3 %copy-start.9 = (s32[512]{0:T(512)S(1)}, s32[512]{0:T(512)}, u32[]{:S(2)}) copy-start(s32[512]{0:T(512)} %param.15) | copy-start | bytes 6148
  346.1 129.5 %all-gather.8.cloned.1.call-start = ((), (), s32[]{:S(2)}) async-start(), calls=%async_computation.8 | async-start | bytes 8519680 | tf_op jit(solution)/shard_map/all_gather | solution.py:141
Sparse Core Ops, SparseCore 0:
  9.1 30.3 all-gather.3
  346.2 22.8 all-gather.5
  386.9 88.5 all-gather.7
where the time goes:
time: 498 us; the launch traced here: 489 us
  waiting for transfers between devices  207 us (42%)
  matrix products  99.6 us (20%)
  blocking collectives  96.2 us (19%)
  starting transfers between devices  37.7 us (8%)
  local copies, waits for them, and re-layouts  28.1 us (6%)
  between operations  13.9 us (3%)
  other arithmetic  5.95 us (1%)
    all_gather x1, waiting for transfers between devices, body(): shard_part = lax.all_gather(embedded, 'seq', axis=0, tiled=True)  87.3 us
    dot_general x12, matrix products, apply_table(): jnp.einsum('ki,qic->qkc', table, values, precision=lax.Precision.HIGHEST)  86.1 us
    all_to_all x1, blocking collectives, long_convolution(): lax.all_to_all(jnp.stack([back_real, back_imag]), 'seq', split_axis=2, co...  57.4 us
    all_to_all x1, waiting for transfers between devices, long_convolution(): lax.all_to_all(outer_forward(filter_blocks), 'seq', split_axis=1, concat_...  46.9 us
    all_gather x1, waiting for transfers between devices, body(): lax.all_gather(mixed, 'ch', axis=1, tiled=True)  23 us
    all_to_all x1, blocking collectives, long_convolution(): lax.all_to_all(result, 'seq', split_axis=0, concat_axis=1, tiled=True)  23 us
    all_to_all x1, waiting for transfers between devices, long_convolution(): lax.all_to_all(outer_forward(signal_blocks), 'seq', split_axis=1, concat_...  18.3 us
    all_gather x1, waiting for transfers between devices, body(): lax.all_gather(features, 'ch', axis=1, tiled=True)  17.4 us
  transfers between devices with their start and end apart: 7, of which 6 were waited for; matrix products, arithmetic and copies ran while one was open for 10% of the time, Pallas kernels for 0%

commit v1 on v0

v1 whole, which is shorter than its diff:
```python
import functools
import math

import jax
import jax.numpy as jnp
import ml_dtypes
import numpy as np
from jax import lax
from jax.experimental import pallas as pl
from jax.experimental.pallas import tpu as pltpu
from jax.sharding import PartitionSpec as P

MESH = pl.DeviceIdType.MESH
LANES = 128
CORES = 2
OWNED = 4
F32 = jnp.float32
BF16 = jnp.bfloat16


def dot(a, b, contract=((1,), (0,))):
    return lax.dot_general(a, b, (contract, ((), ())), preferred_element_type=F32)


def split(values):
    high = values.astype(BF16)
    return high, (values - high.astype(F32)).astype(BF16)


def split_table(values):
    high = values.astype(ml_dtypes.bfloat16)
    return np.stack([high, (values - high.astype(np.float64)).astype(ml_dtypes.bfloat16)])


def transform_tables(blocks):
    length = blocks * LANES
    shifted = np.arange(blocks, dtype=np.float64) + 0.25
    outer = 2.0 * math.pi * shifted[:, None] * np.arange(blocks)[None, :] / blocks
    first = np.concatenate([np.cos(outer), -np.sin(outer)], axis=0)
    twist = 2.0 * math.pi * shifted[:, None] * np.arange(LANES)[None, :] / length
    lane = np.arange(LANES)
    inner = 2.0 * math.pi * (lane[:, None] * lane[None, :] % LANES) / LANES
    second = np.block([[np.cos(inner), -np.sin(inner)], [np.sin(inner), np.cos(inner)]])
    return (
        split_table(first),
        np.stack([np.cos(twist), np.sin(twist)]).astype(np.float32),
        split_table(second),
        split_table(second.T),
        split_table(first.T / length),
    )


def exact3(data, table, data_left=True):
    high, low = split(data)
    if data_left:
        return dot(high, table[0]) + dot(low, table[0]) + dot(high, table[1])
    return dot(table[0], high) + dot(table[0], low) + dot(table[1], high)


def side_by_side(parts):
    return jnp.concatenate(parts, axis=1)


def forward(values, first, twist, second):
    blocks = values.shape[0]
    stage = dot(first[0], values) + dot(first[1], values)
    real, imag = stage[:blocks], stage[blocks:]
    cos, sin = twist[0], twist[1]
    rows = []
    for c in range(OWNED):
        lanes = slice(c * LANES, (c + 1) * LANES)
        r, i = real[:, lanes], imag[:, lanes]
        rows.append(side_by_side([r * cos + i * sin, i * cos - r * sin]))
    return exact3(jnp.concatenate(rows, axis=0), second)


def multiply(a, b):
    ar, ai, br, bi = a[:, :LANES], a[:, LANES:], b[:, :LANES], b[:, LANES:]
    return side_by_side([ar * br - ai * bi, ar * bi + ai * br])


def backward(spectrum, last, twist, second):
    blocks = spectrum.shape[0] // OWNED
    stage = exact3(spectrum, second)
    cos, sin = twist[0], twist[1]
    real, imag = [], []
    for c in range(OWNED):
        rows = stage[c * blocks : (c + 1) * blocks]
        r, i = rows[:, :LANES], rows[:, LANES:]
        real.append(r * cos - i * sin)
        imag.append(i * cos + r * sin)
    return exact3(
        jnp.concatenate([side_by_side(real), side_by_side(imag)], axis=0), last, data_left=False
    )


def layer_kernel(
    sizes,
    features, w_in, bias, filters, w_out, w_emb, lengths, owners,
    first_t, twist_t, second_t, second_back_t, last_t,
    out,
    feat, w_vm, w_turned, filt_vm, w_out_vm, w_emb_vm, first_v, twist_v, second_v, second_back_v, last_v,
    stage, filt_send, filt_recv, sig_send, sig_recv, conv_send, conv_recv,
    signal_t, gate_t, spectrum, term_send, term_recv, weight_high, weight_low,
    emb_send, emb_recv, table, chosen, contrib, from_core, joined, joined_recv,
    local_sem, feat_send_sem, feat_recv_sem, turn_send_sem, turn_recv_sem,
    term_send_sem, term_recv_sem, emb_send_sem, emb_recv_sem,
    z_send_sem, z_recv_sem, y_send_sem, y_recv_sem, core_sem, join_send_sem, join_recv_sem,
):
    seq_n, ch_n, y_n, z_n = sizes
    rows_dev, chan_dev = filters.shape
    quads = rows_dev // LANES
    pack = quads * OWNED
    blocks = seq_n * quads
    part_rows = rows_dev // ch_n
    me, ch = lax.axis_index("seq"), lax.axis_index("ch")
    core = lax.rem(me, CORES)
    place = lax.div(me, CORES)
    my_z = lax.rem(place, z_n)
    my_y = lax.div(place, z_n)

    def seq_peer(i):
        return lax.rem(me + i, seq_n)

    def ch_peer(i):
        return lax.rem(ch + i, ch_n)

    barrier = pltpu.get_barrier_semaphore()

    @pl.loop(1, seq_n)
    def _(i):
        pl.semaphore_signal(barrier, inc=1, device_id=(seq_peer(i), ch), device_id_type=MESH)

    for i in range(1, ch_n):
        pl.semaphore_signal(barrier, inc=1, device_id=(me, ch_peer(i)), device_id_type=MESH)

    loads = [
        (filters, filt_vm), (w_in, w_vm), (features, feat.at[ch]), (first_t, first_v), (twist_t, twist_v),
        (second_t, second_v), (w_out, w_out_vm), (w_emb, w_emb_vm), (second_back_t, second_back_v), (last_t, last_v),
    ]
    loads = [pltpu.make_async_copy(a, b, local_sem.at[n]) for n, (a, b) in enumerate(loads)]
    for load in loads:
        load.start()

    def scatter(send, recv, n):
        @pl.loop(1, seq_n)
        def _(i):
            peer = seq_peer(i)
            pltpu.make_async_remote_copy(
                src_ref=send.at[pl.ds(pl.multiple_of(peer * pack, pack), pack)],
                dst_ref=recv.at[pl.ds(pl.multiple_of(me * pack, pack), pack)],
                send_sem=turn_send_sem.at[n],
                recv_sem=turn_recv_sem.at[n],
                device_id=(peer, ch),
                device_id_type=MESH,
            ).start()

        mine = pl.ds(pl.multiple_of(me * pack, pack), pack)
        recv[mine] = send[mine]

    def gathered(send, recv, n):
        most = pl.ds(0, (seq_n - 1) * pack)
        whole = pltpu.make_async_remote_copy(
            src_ref=send.at[most], dst_ref=recv.at[most], send_sem=turn_send_sem.at[n],
            recv_sem=turn_recv_sem.at[n], device_id=(seq_peer(1), ch), device_id_type=MESH,
        )
        whole.wait_send()
        whole.wait_recv()

    def chunks_by_channel(turned, send):
        for q in range(quads):
            for c in range(OWNED):
                stage[pl.ds(q * OWNED + c, seq_n, pack), :] = turned[
                    c * seq_n : (c + 1) * seq_n, q * LANES : (q + 1) * LANES
                ]
        send[...] = stage[...].astype(BF16)

    def whole_document(recv):
        stage[...] = recv[...].astype(F32)
        return side_by_side([stage[pl.ds(c, blocks, OWNED), :] for c in range(OWNED)]).astype(BF16)

    loads[0].wait()
    chunks_by_channel(filt_vm[...].T, filt_send)
    loads[1].wait()
    for b in range(3):
        w_turned[b] = w_vm[b].T

    pl.semaphore_wait(barrier, seq_n - 1 + ch_n - 1)
    loads[2].wait()

    def feature_copy(i):
        return pltpu.make_async_remote_copy(
            src_ref=feat.at[ch], dst_ref=feat.at[ch], send_sem=feat_send_sem.at[i], recv_sem=feat_recv_sem.at[i],
            device_id=(me, ch_peer(i)), device_id_type=MESH,
        )

    for i in (1, ch_n - 1, *range(2, ch_n - 1)) if ch_n > 2 else (1,):
        feature_copy(i).start()
    scatter(filt_send, filt_recv, 0)

    loads[6].wait()
    loads[7].wait()
    emb_turned = w_emb_vm[...].astype(F32).T.astype(BF16)
    term = dot(emb_turned, w_out_vm[...], ((1,), (1,)))
    for c in range(ch_n):
        term_send[c] = term[:, c * chan_dev : (c + 1) * chan_dev]

    def add_projection(source, first_time):
        block = feat[source]
        for b in range(3):
            lanes = pl.ds(pl.multiple_of(source * chan_dev, chan_dev), chan_dev)
            product = dot(w_turned[b, :, lanes], block, ((1,), (1,)))
            target = (gate_t, signal_t, spectrum)[b]
            if b == 2:
                view = pl.ds(0, chan_dev)
                for q in range(2):
                    lanes2 = slice(q * 2 * LANES, (q + 1) * 2 * LANES)
                    rows = pl.ds(q * chan_dev, chan_dev)
                    if first_time:
                        spectrum[rows, :] = product[:, lanes2]
                    else:
                        spectrum[rows, :] += product[:, lanes2]
            elif first_time:
                target[...] = product
            else:
                target[...] += product

    add_projection(ch, True)
    for i in (1, ch_n - 1, *range(2, ch_n - 1)) if ch_n > 2 else (1,):
        feature_copy(i).wait_recv()
        add_projection(lax.rem(ch + ch_n - i, ch_n), False)
    value = side_by_side([spectrum[:chan_dev, :], spectrum[chan_dev : 2 * chan_dev, :]])
    signal_t[...] = signal_t[...] * value
    chunks_by_channel(signal_t[...], sig_send)
    scatter(sig_send, sig_recv, 1)

    def term_copy(i):
        return pltpu.make_async_remote_copy(
            src_ref=term_send.at[ch_peer(i)], dst_ref=term_recv.at[ch], send_sem=term_send_sem.at[i],
            recv_sem=term_recv_sem.at[i], device_id=(me, ch_peer(i)), device_id_type=MESH,
        )

    for i in range(1, ch_n):
        term_copy(i).start()
    term_recv[ch] = term_send[ch]

    gathered(filt_send, filt_recv, 0)
    for n in (3, 4, 5):
        loads[n].wait()
    spectrum[...] = forward(whole_document(filt_recv), first_v, twist_v, second_v)

    pages = lengths.shape[1]
    length_row = lengths[...].astype(F32)
    owner_row = owners[...].astype(F32)
    length_col = jnp.broadcast_to(length_row, (LANES, pages)).T
    owner_col = side_by_side([jnp.broadcast_to(owner_row, (LANES, pages)).T] * (pages // LANES))
    here = lax.broadcasted_iota(jnp.int32, (pages, pages), 0)
    other = lax.broadcasted_iota(jnp.int32, (pages, pages), 1)
    earlier = jnp.where(other < here, 1.0, 0.0)
    ahead = jnp.where(owner_row < owner_col, 1.0, jnp.where(owner_row == owner_col, earlier, 0.0))
    length_b = length_col.astype(BF16)
    placed = dot(ahead.astype(BF16), length_b)
    move = dot(earlier.astype(BF16), length_b) - placed
    move_high = jnp.floor(move * (1.0 / 256.0))
    move_low = (move - 256.0 * move_high).astype(BF16)
    placed_row = placed.T[0:1]
    chip_rows = CORES * rows_dev
    row0 = place * chip_rows
    position = (lax.broadcasted_iota(jnp.int32, (chip_rows, pages), 0) + row0).astype(F32)
    inside = jnp.where(position >= placed_row, jnp.where(position < placed_row + length_row, 1.0, 0.0), 0.0)
    inside = inside.astype(BF16)
    source = (
        position[:, :LANES] + 256.0 * dot(inside, move_high.astype(BF16)) + dot(inside, move_low)
    ).astype(jnp.int32)
    in_part = source & (part_rows - 1)
    token_part = (source >> int(math.log2(part_rows))) & (ch_n - 1)
    token_core = (source >> int(math.log2(rows_dev))) & (CORES - 1)
    token_place = source >> int(math.log2(chip_rows))
    slot = jnp.where(token_part == ch, jnp.where(token_core == core, token_place * part_rows + in_part, -1), -1)
    lane = lax.broadcasted_iota(jnp.int32, (chip_rows, LANES), 1)
    for b in range(chosen.shape[1] // LANES):
        chosen[:, b * LANES : (b + 1) * LANES] = jnp.where(slot == lane + b * LANES, 1.0, 0.0).astype(BF16)

    gathered(sig_send, sig_recv, 1)
    product = multiply(forward(whole_document(sig_recv), first_v, twist_v, second_v), spectrum[...])
    for n in (8, 9):
        loads[n].wait()
    convolved = backward(product, last_v, twist_v, second_back_v)
    for c in range(OWNED):
        stage[pl.ds(c, blocks, OWNED), :] = convolved[:, c * LANES : (c + 1) * LANES]
    conv_send[...] = stage[...].astype(BF16)
    scatter(conv_send, conv_recv, 2)

    for i in range(1, ch_n):
        term_copy(i).wait_recv()
    weight = term_recv[0]
    for c in range(1, ch_n):
        weight = weight + term_recv[c]
    weight_high[...], weight_low[...] = split(weight)
    own_part = dot(emb_turned, feat[ch], ((1,), (1,)))
    bias_col = side_by_side([jnp.broadcast_to(bias[...], (LANES, chan_dev)).T] * quads)
    skipped = bias_col * signal_t[...]

    gathered(conv_send, conv_recv, 2)
    stage[...] = conv_recv[...].astype(F32)
    convolved_t = jnp.concatenate(
        [
            side_by_side([stage[pl.ds(q * OWNED + c, seq_n, pack), :] for q in range(quads)])
            for c in range(OWNED)
        ],
        axis=0,
    )
    mixed = ((convolved_t + skipped) * gate_t[...]).astype(BF16)
    embedded = (dot(weight_high[...], mixed) + dot(weight_low[...], mixed) + own_part).T
    for c in range(ch_n):
        emb_send[c] = embedded[c * part_rows : (c + 1) * part_rows]

    def emb_copy(i):
        return pltpu.make_async_remote_copy(
            src_ref=emb_send.at[ch_peer(i)], dst_ref=emb_recv.at[ch], send_sem=emb_send_sem.at[i],
            recv_sem=emb_recv_sem.at[i], device_id=(me, ch_peer(i)), device_id_type=MESH,
        )

    for i in range(1, ch_n):
        emb_copy(i).start()
    emb_recv[ch] = emb_send[ch]
    for i in range(1, ch_n):
        emb_copy(i).wait_recv()
    total = emb_recv[0]
    for c in range(1, ch_n):
        total = total + emb_recv[c]
    table[place] = total.astype(BF16)

    def seq_of(y, z, k):
        return (y * z_n + z) * CORES + k

    def z_copy(i):
        return pltpu.make_async_remote_copy(
            src_ref=table.at[place], dst_ref=table.at[place], send_sem=z_send_sem.at[i], recv_sem=z_recv_sem.at[i],
            device_id=(seq_of(my_y, lax.rem(my_z + i, z_n), core), ch), device_id_type=MESH,
        )

    def y_copy(i, j):
        spot = my_y * z_n + lax.rem(my_z + z_n - j, z_n)
        return pltpu.make_async_remote_copy(
            src_ref=table.at[spot], dst_ref=table.at[spot], send_sem=y_send_sem.at[i, j], recv_sem=y_recv_sem.at[i, j],
            device_id=(seq_of(lax.rem(my_y + i, y_n), my_z, core), ch), device_id_type=MESH,
        )

    order = sorted(range(1, z_n), key=lambda i: min(i, z_n - i))
    for i in order:
        z_copy(i).start()
    for j in [0, *order]:
        if j:
            z_copy(j).wait_recv()
        for i in range(1, y_n):
            y_copy(i, j).start()
    for j in [0, *order]:
        for i in range(1, y_n):
            y_copy(i, j).wait_recv()

    @pl.loop(0, CORES)
    def _(k):
        rows = pl.ds(pl.multiple_of(k * rows_dev, rows_dev), rows_dev)
        stack = table[...].reshape(y_n * z_n * part_rows, LANES)
        contrib[k] = dot(chosen[rows, :], stack).astype(BF16)

    partner = me + 1 - 2 * core
    swap = pltpu.make_async_remote_copy(
        src_ref=contrib.at[1 - core], dst_ref=from_core, send_sem=core_sem.at[0], recv_sem=core_sem.at[1],
        device_id=(partner, ch), device_id_type=MESH,
    )
    swap.start()
    swap.wait_recv()
    joined[...] = contrib[core] + from_core[...]

    def join_copy(i):
        return pltpu.make_async_remote_copy(
            src_ref=joined, dst_ref=joined_recv.at[ch], send_sem=join_send_sem.at[i], recv_sem=join_recv_sem.at[i],
            device_id=(me, ch_peer(i)), device_id_type=MESH,
        )

    for i in range(1, ch_n):
        join_copy(i).start()
    result = joined[...]
    for i in range(1, ch_n):
        join_copy(i).wait_recv()
        result = result + joined_recv[lax.rem(ch + ch_n - i, ch_n)]
    out[...] = result

    swap.wait_send()
    for i in range(1, ch_n):
        feature_copy(i).wait_send()
        term_copy(i).wait_send()
        emb_copy(i).wait_send()
        join_copy(i).wait_send()
    for i in order:
        z_copy(i).wait_send()
    for j in [0, *order]:
        for i in range(1, y_n):
            y_copy(i, j).wait_send()


def body(sizes, features, w_in, bias_skip, filters, w_out, w_emb, page_lengths, page_owner):
    seq_n, ch_n, y_n, z_n = sizes
    rows_dev, chan_dev = features.shape
    width, emb = w_out.shape[0], w_emb.shape[1]
    quads = rows_dev // LANES
    blocks = seq_n * quads
    turn_rows = seq_n * quads * OWNED
    part_rows = rows_dev // ch_n
    places = y_n * z_n
    tables = [jnp.asarray(t) for t in transform_tables(blocks)]
    vmem, sem = pltpu.VMEM, pltpu.SemaphoreType.DMA
    turn = vmem((turn_rows, LANES), BF16)
    scratch = [
        vmem((ch_n, rows_dev, chan_dev), BF16),
        vmem((3, width, chan_dev), BF16),
        vmem((3, chan_dev, width), BF16),
        vmem((rows_dev, chan_dev), F32),
        vmem(w_out.shape, BF16),
        vmem(w_emb.shape, BF16),
        *(vmem(t.shape, t.dtype) for t in tables),
        vmem((turn_rows, LANES), F32),
        *([turn] * 6),
        vmem((chan_dev, rows_dev), F32),
        vmem((chan_dev, rows_dev), F32),
        vmem((OWNED * blocks, 2 * LANES), F32),
        vmem((ch_n, emb, chan_dev), F32),
        vmem((ch_n, emb, chan_dev), F32),
        vmem((emb, chan_dev), BF16),
        vmem((emb, chan_dev), BF16),
        vmem((ch_n, part_rows, emb), F32),
        vmem((ch_n, part_rows, emb), F32),
        vmem((places, part_rows, emb), BF16),
        vmem((CORES * rows_dev, places * part_rows), BF16),
        vmem((CORES, rows_dev, emb), BF16),
        vmem((rows_dev, emb), BF16),
        vmem((rows_dev, emb), BF16),
        vmem((ch_n, rows_dev, emb), BF16),
        sem((10,)),
        sem((ch_n,)), sem((ch_n,)),
        sem((3,)), sem((3,)),
        sem((ch_n,)), sem((ch_n,)),
        sem((ch_n,)), sem((ch_n,)),
        sem((z_n,)), sem((z_n,)),
        sem((y_n, z_n)), sem((y_n, z_n)),
        sem((2,)),
        sem((ch_n,)), sem((ch_n,)),
    ]
    anywhere = pl.BlockSpec(memory_space=pl.ANY)
    inside = pl.BlockSpec(memory_space=pltpu.VMEM)
    return pl.pallas_call(
        functools.partial(layer_kernel, sizes),
        out_shape=jax.ShapeDtypeStruct((rows_dev, emb), BF16),
        in_specs=[anywhere, anywhere, inside, anywhere, anywhere, anywhere, inside, inside] + [anywhere] * 5,
        out_specs=inside,
        scratch_shapes=scratch,
        compiler_params=pltpu.CompilerParams(
            collective_id=0, has_side_effects=True, vmem_limit_bytes=60 * 1024 * 1024
        ),
        name="hyena_layer",
    )(
        features,
        jnp.transpose(w_in, (1, 0, 2)),
        bias_skip[None, :],
        filters,
        w_out,
        w_emb,
        page_lengths[None, :],
        page_owner[None, :],
        *tables,
    )


def solution(mesh):
    seq_n, ch_n = mesh.shape["seq"], mesh.shape["ch"]
    places = seq_n // CORES
    z_n = min(8, max(1, places // 2))
    sizes = (seq_n, ch_n, places // z_n, z_n)
    return jax.shard_map(
        functools.partial(body, sizes),
        mesh=mesh,
        in_specs=(
            P("seq", "ch"),
            P(None, None, "ch"),
            P("ch"),
            P("seq", "ch"),
            P(None, "ch"),
            P("ch", None),
            P(),
            P(),
        ),
        out_specs=P("seq", None),
        check_vma=False,
    )
```

time: 498 us -> 85.7 us (0.17); the launches traced: 489 us -> 85.6 us
  waiting for transfers between devices: 207 us -> 0 us
  matrix products: 99.6 us -> 0 us
  blocking collectives: 96.2 us -> 0 us
  Pallas kernels: 0 us -> 84 us
  starting transfers between devices: 37.7 us -> 0 us
  local copies, waits for them, and re-layouts: 28.1 us -> 1.57 us
  between operations: 13.9 us -> 0.01 us
  other arithmetic: 5.95 us -> 0 us
    all_gather x3 -> x0, waiting for transfers between devices: 128 us -> none  [the longest x1 87.3 us: body(): shard_part = lax.all_gather(embedded, 'seq', axis=0, tiled=True)]
    dot_general x20 -> x0, matrix products: 99.6 us -> none  [the longest x12 86.1 us: apply_table(): jnp.einsum('ki,qic->qkc', table, values, precision=lax.Precision.HIGHEST)]
    pallas_call x0 -> x1, Pallas kernels: none -> 84 us  [body(): pl.pallas_call(functools.partial(layer_kernel, sizes), out_shape=jax.Shap...]
    all_to_all x2 -> x0, blocking collectives: 80.3 us -> none  [the longest x1 57.4 us: long_convolution(): lax.all_to_all(jnp.stack([back_real, back_imag]), 'seq', split_axis=2, co...]
    all_to_all x4 -> x0, waiting for transfers between devices: 79 us -> none  [the longest x1 46.9 us: long_convolution(): lax.all_to_all(outer_forward(filter_blocks), 'seq', split_axis=1, concat_...]
    all_to_all x4 -> x0, starting transfers between devices: 37.6 us -> none  [the longest x1 13.2 us: long_convolution(): lax.all_to_all(filters.reshape(seq_count, group_rows, chan_dev), 'seq', s...]
    psum x1 -> x0, blocking collectives: 15.8 us -> none  [body(): lax.psum(jnp.dot(layer_out, w_emb, preferred_element_type=jnp.float32), '...]
    another operation x4 -> x0, local copies, waits for them, and re-layouts: 7.68 us -> none  [the longest x2 5.09 us: outer_forward(): jnp.stack([real_part * twist_cos + imag_part * twist_sin, imag_part * twi...]
  transfers between devices with their start and end apart: 7 -> 0, of which waited for: 6 -> 0; matrix products, arithmetic and copies ran while one was open for 10% -> 0% of each run, Pallas kernels for 0% -> 0%
where the time goes in v1:
time: 85.7 us; the launch traced here: 85.6 us
  Pallas kernels  84 us (98%)
  local copies, waits for them, and re-layouts  1.57 us (2%)
    pallas_call x1, Pallas kernels, body(): pl.pallas_call(functools.partial(layer_kernel, sizes), out_shape=jax.Shap...  84 us

profile of v1, /device:TPU:1, one launch (start us, length us, event | category | flops | bytes accessed | tf_op | source)
XLA Modules:
  0.0 85.6 jit_solution(371038560327452557)
XLA Ops:
  0.0 84.0 %hyena_layer.1 = bf16[512,128]{1,0:T(8,128)(2,1)} custom-call(bf16[512,256]{1,0:T(8,128)(2,1)} %features.1, bf16[3,1024,256]{2,1,0:T(8,128)(2,1)} %bitcast.4, f32[1,256]{1,0:T(1,128)} %bitcast.7, f32[512,256]{1,0:T(8,128)} %filters.1, bf16[1024,256]{1,0:T(8,128)(2,1)} %w_out.1, bf16[256,128]{1,0:T(8,128)(2,1)} %w_emb.1, s32[1,512]{1,0:T(1,128)} %bitcast.5, ...), custom_call_target="tpu_custom_call" | custom-call | tf_op jit(solution)/shard_map/hyena_layer/pallas_call | solution.py:453
  84.1 1.6 %copy.15 = bf16[512,128]{1,0:T(8,128)(2,1)} copy(bf16[512,128]{1,0:T(8,128)(2,1)} %hyena_layer.1) | data formatting | bytes 262144

commit v2 on v1

--- a/solution.py
+++ b/solution.py
@@ -11,6 +11,7 @@
 from jax.sharding import PartitionSpec as P
 
 MESH = pl.DeviceIdType.MESH
+RING = ("right_low", "right_high", "left_high", "left_low", "right_on", "left_on")
 LANES = 128
 CORES = 2
 OWNED = 4
@@ -102,28 +103,33 @@
     feat, w_vm, w_turned, filt_vm, w_out_vm, w_emb_vm, first_v, twist_v, second_v, second_back_v, last_v,
     stage, filt_send, filt_recv, sig_send, sig_recv, conv_send, conv_recv,
     signal_t, gate_t, spectrum, term_send, term_recv, weight_high, weight_low,
-    emb_send, emb_recv, table, chosen, contrib, from_core, joined, joined_recv,
+    emb_send, emb_recv, map_send, map_recv, chosen, col_send, col_recv, out_send, out_recv, joined,
     local_sem, feat_send_sem, feat_recv_sem, turn_send_sem, turn_recv_sem,
     term_send_sem, term_recv_sem, emb_send_sem, emb_recv_sem,
-    z_send_sem, z_recv_sem, y_send_sem, y_recv_sem, core_sem, join_send_sem, join_recv_sem,
+    join_send_sem, join_recv_sem,
 ):
-    seq_n, ch_n, y_n, z_n = sizes
+    seq_n, ch_n = sizes
     rows_dev, chan_dev = filters.shape
     quads = rows_dev // LANES
     pack = quads * OWNED
     blocks = seq_n * quads
-    part_rows = rows_dev // ch_n
+    places = seq_n // CORES
+    share = w_emb.shape[1] // ch_n
     me, ch = lax.axis_index("seq"), lax.axis_index("ch")
     core = lax.rem(me, CORES)
     place = lax.div(me, CORES)
-    my_z = lax.rem(place, z_n)
-    my_y = lax.div(place, z_n)
 
     def seq_peer(i):
         return lax.rem(me + i, seq_n)
 
     def ch_peer(i):
         return lax.rem(ch + i, ch_n)
+
+    sent = []
+
+    def go(copy):
+        copy.start()
+        sent.append(copy)
 
     barrier = pltpu.get_barrier_semaphore()
 
@@ -158,14 +164,32 @@
         mine = pl.ds(pl.multiple_of(me * pack, pack), pack)
         recv[mine] = send[mine]
 
+    def same_core(src_of, dst_of, n):
+        @pl.loop(1, places)
+        def _(i):
+            peer = lax.rem(place + i, places)
+            pltpu.make_async_remote_copy(
+                src_ref=src_of(peer), dst_ref=dst_of(), send_sem=turn_send_sem.at[n], recv_sem=turn_recv_sem.at[n],
+                device_id=(peer * CORES + core, ch), device_id_type=MESH,
+            ).start()
+
+    def all_in(recv, copies, n):
+        most = recv.at[pl.ds(0, copies)]
+        whole = pltpu.make_async_remote_copy(
+            src_ref=most, dst_ref=most, send_sem=turn_send_sem.at[n],
+            recv_sem=turn_recv_sem.at[n], device_id=(seq_peer(1), ch), device_id_type=MESH,
+        )
+        whole.wait_recv()
+        sent.append(whole)
+
     def gathered(send, recv, n):
         most = pl.ds(0, (seq_n - 1) * pack)
         whole = pltpu.make_async_remote_copy(
             src_ref=send.at[most], dst_ref=recv.at[most], send_sem=turn_send_sem.at[n],
             recv_sem=turn_recv_sem.at[n], device_id=(seq_peer(1), ch), device_id_type=MESH,
         )
-        whole.wait_send()
         whole.wait_recv()
+        sent.append(whole)
 
     def chunks_by_channel(turned, send):
         for q in range(quads):
@@ -179,6 +203,36 @@
         stage[...] = recv[...].astype(F32)
         return side_by_side([stage[pl.ds(c, blocks, OWNED), :] for c in range(OWNED)]).astype(BF16)
 
+    pages = lengths.shape[1]
+    length_row = lengths[...].astype(F32)
+    owner_row = owners[...].astype(F32)
+    length_col = jnp.broadcast_to(length_row, (LANES, pages)).T
+    owner_col = side_by_side([jnp.broadcast_to(owner_row, (LANES, pages)).T] * (pages // LANES))
+    here = lax.broadcasted_iota(jnp.int32, (pages, pages), 0)
+    other = lax.broadcasted_iota(jnp.int32, (pages, pages), 1)
+    earlier = jnp.where(other < here, 1.0, 0.0)
+    ahead = jnp.where(owner_row < owner_col, 1.0, jnp.where(owner_row == owner_col, earlier, 0.0))
+    length_b = length_col.astype(BF16)
+    placed = dot(ahead.astype(BF16), length_b)
+    move = dot(earlier.astype(BF16), length_b) - placed
+    move_high = jnp.floor(move * (1.0 / 256.0))
+    move_low = move - 256.0 * move_high
+    begin = side_by_side([placed] * quads)
+    end = side_by_side([placed + length_col] * quads)
+    position = (lax.broadcasted_iota(jnp.int32, (pages, rows_dev), 1) + me * rows_dev).astype(F32)
+    inside = jnp.where(position >= begin, jnp.where(position < end, 1.0, 0.0), 0.0).astype(BF16)
+    source = (
+        position[:16]
+        + 256.0 * dot(move_high.T[:16].astype(BF16), inside)
+        + dot(move_low.T[:16].astype(BF16), inside)
+    )
+    source_block = jnp.floor(source * (1.0 / LANES))
+    source_lane = source - LANES * source_block
+    for q in range(quads):
+        lanes = slice(q * LANES, (q + 1) * LANES)
+        map_send[q : q + 1, :] = source_block[:1, lanes]
+        map_send[quads + q : quads + q + 1, :] = source_lane[:1, lanes]
+
     loads[0].wait()
     chunks_by_channel(filt_vm[...].T, filt_send)
     loads[1].wait()
@@ -188,16 +242,39 @@
     pl.semaphore_wait(barrier, seq_n - 1 + ch_n - 1)
     loads[2].wait()
 
-    def feature_copy(i):
+    def ring_copy(held, left, right, sems, rows, kind):
+        (lane_of, send_sem, recv_sem) = sems
+        half = rows // 2
+        own, spot, top, device = {
+            "right_low": (1, 1, 0, right), "right_high": (1, 1, 1, right),
+            "left_high": (1, 1, 1, left), "left_low": (1, 1, 0, left),
+            "right_on": (0, 0, 0, right), "left_on": (0, 2, 1, left),
+        }[kind]
+        block = held(spot).at[pl.ds(top * half, half)]
+        n = RING.index(kind)
         return pltpu.make_async_remote_copy(
-            src_ref=feat.at[ch], dst_ref=feat.at[ch], send_sem=feat_send_sem.at[i], recv_sem=feat_recv_sem.at[i],
-            device_id=(me, ch_peer(i)), device_id_type=MESH,
-        )
-
-    for i in (1, ch_n - 1, *range(2, ch_n - 1)) if ch_n > 2 else (1,):
-        feature_copy(i).start()
+            src_ref=block, dst_ref=block, send_sem=send_sem.at[(*lane_of, n)], recv_sem=recv_sem.at[(*lane_of, n)],
+            device_id=device, device_id_type=MESH,
+        )
+
+    def feature_copy(kind):
+        return ring_copy(
+            lambda spot: feat.at[lax.rem(ch + ch_n - 1 + spot, ch_n)], (me, ch_peer(ch_n - 1)), (me, ch_peer(1)),
+            ((), feat_send_sem, feat_recv_sem), rows_dev, kind,
+        )
+
+    ring_first = RING[:4] if ch_n == 4 else RING[:2]
+    for kind in ring_first:
+        go(feature_copy(kind))
+
     scatter(filt_send, filt_recv, 0)
-
+    map_recv[place] = map_send[...]
+    same_core(lambda peer: map_send, lambda: map_recv.at[place], 3)
+    if ch_n == 4:
+        feature_copy("right_low").wait_recv()
+        go(feature_copy("right_on"))
+        feature_copy("left_high").wait_recv()
+        go(feature_copy("left_on"))
     loads[6].wait()
     loads[7].wait()
     emb_turned = w_emb_vm[...].astype(F32).T.astype(BF16)
@@ -226,9 +303,18 @@
                 target[...] += product
 
     add_projection(ch, True)
-    for i in (1, ch_n - 1, *range(2, ch_n - 1)) if ch_n > 2 else (1,):
-        feature_copy(i).wait_recv()
-        add_projection(lax.rem(ch + ch_n - i, ch_n), False)
+    if ch_n == 4:
+        feature_copy("right_high").wait_recv()
+        add_projection(ch_peer(3), False)
+        feature_copy("left_low").wait_recv()
+        add_projection(ch_peer(1), False)
+        feature_copy("right_on").wait_recv()
+        feature_copy("left_on").wait_recv()
+        add_projection(ch_peer(2), False)
+    elif ch_n == 2:
+        for kind in ring_first:
+            feature_copy(kind).wait_recv()
+        add_projection(ch_peer(1), False)
     value = side_by_side([spectrum[:chan_dev, :], spectrum[chan_dev : 2 * chan_dev, :]])
     signal_t[...] = signal_t[...] * value
     chunks_by_channel(signal_t[...], sig_send)
@@ -241,45 +327,13 @@
         )
 
     for i in range(1, ch_n):
-        term_copy(i).start()
+        go(term_copy(i))
     term_recv[ch] = term_send[ch]
 
     gathered(filt_send, filt_recv, 0)
     for n in (3, 4, 5):
         loads[n].wait()
     spectrum[...] = forward(whole_document(filt_recv), first_v, twist_v, second_v)
-
-    pages = lengths.shape[1]
-    length_row = lengths[...].astype(F32)
-    owner_row = owners[...].astype(F32)
-    length_col = jnp.broadcast_to(length_row, (LANES, pages)).T
-    owner_col = side_by_side([jnp.broadcast_to(owner_row, (LANES, pages)).T] * (pages // LANES))
-    here = lax.broadcasted_iota(jnp.int32, (pages, pages), 0)
-    other = lax.broadcasted_iota(jnp.int32, (pages, pages), 1)
-    earlier = jnp.where(other < here, 1.0, 0.0)
-    ahead = jnp.where(owner_row < owner_col, 1.0, jnp.where(owner_row == owner_col, earlier, 0.0))
-    length_b = length_col.astype(BF16)
-    placed = dot(ahead.astype(BF16), length_b)
-    move = dot(earlier.astype(BF16), length_b) - placed
-    move_high = jnp.floor(move * (1.0 / 256.0))
-    move_low = (move - 256.0 * move_high).astype(BF16)
-    placed_row = placed.T[0:1]
-    chip_rows = CORES * rows_dev
-    row0 = place * chip_rows
-    position = (lax.broadcasted_iota(jnp.int32, (chip_rows, pages), 0) + row0).astype(F32)
-    inside = jnp.where(position >= placed_row, jnp.where(position < placed_row + length_row, 1.0, 0.0), 0.0)
-    inside = inside.astype(BF16)
-    source = (
-        position[:, :LANES] + 256.0 * dot(inside, move_high.astype(BF16)) + dot(inside, move_low)
-    ).astype(jnp.int32)
-    in_part = source & (part_rows - 1)
-    token_part = (source >> int(math.log2(part_rows))) & (ch_n - 1)
-    token_core = (source >> int(math.log2(rows_dev))) & (CORES - 1)
-    token_place = source >> int(math.log2(chip_rows))
-    slot = jnp.where(token_part == ch, jnp.where(token_core == core, token_place * part_rows + in_part, -1), -1)
-    lane = lax.broadcasted_iota(jnp.int32, (chip_rows, LANES), 1)
-    for b in range(chosen.shape[1] // LANES):
-        chosen[:, b * LANES : (b + 1) * LANES] = jnp.where(slot == lane + b * LANES, 1.0, 0.0).astype(BF16)
 
     gathered(sig_send, sig_recv, 1)
     product = multiply(forward(whole_document(sig_recv), first_v, twist_v, second_v), spectrum[...])
@@ -297,6 +351,14 @@
     for c in range(1, ch_n):
         weight = weight + term_recv[c]
     weight_high[...], weight_low[...] = split(weight)
+    all_in(map_recv, places - 1, 3)
+    block_row = lax.broadcasted_iota(jnp.int32, (blocks, rows_dev), 0).astype(F32)
+
+    @pl.loop(0, places)
+    def _(d):
+        row = side_by_side([map_recv[d, q : q + 1, :] for q in range(quads)])
+        chosen[d] = jnp.where(block_row == row, 1.0, 0.0).astype(BF16)
+
     own_part = dot(emb_turned, feat[ch], ((1,), (1,)))
     bias_col = side_by_side([jnp.broadcast_to(bias[...], (LANES, chan_dev)).T] * quads)
     skipped = bias_col * signal_t[...]
@@ -311,9 +373,9 @@
         axis=0,
     )
     mixed = ((convolved_t + skipped) * gate_t[...]).astype(BF16)
-    embedded = (dot(weight_high[...], mixed) + dot(weight_low[...], mixed) + own_part).T
+    embedded = (dot(weight_high[...], mixed) + dot(weight_low[...], mixed) + own_part)
     for c in range(ch_n):
-        emb_send[c] = embedded[c * part_rows : (c + 1) * part_rows]
+        emb_send[c] = embedded[c * share : (c + 1) * share]
 
     def emb_copy(i):
         return pltpu.make_async_remote_copy(
@@ -322,94 +384,74 @@
         )
 
     for i in range(1, ch_n):
-        emb_copy(i).start()
+        go(emb_copy(i))
     emb_recv[ch] = emb_send[ch]
     for i in range(1, ch_n):
         emb_copy(i).wait_recv()
     total = emb_recv[0]
     for c in range(1, ch_n):
         total = total + emb_recv[c]
-    table[place] = total.astype(BF16)
-
-    def seq_of(y, z, k):
-        return (y * z_n + z) * CORES + k
-
-    def z_copy(i):
-        return pltpu.make_async_remote_copy(
-            src_ref=table.at[place], dst_ref=table.at[place], send_sem=z_send_sem.at[i], recv_sem=z_recv_sem.at[i],
-            device_id=(seq_of(my_y, lax.rem(my_z + i, z_n), core), ch), device_id_type=MESH,
-        )
-
-    def y_copy(i, j):
-        spot = my_y * z_n + lax.rem(my_z + z_n - j, z_n)
-        return pltpu.make_async_remote_copy(
-            src_ref=table.at[spot], dst_ref=table.at[spot], send_sem=y_send_sem.at[i, j], recv_sem=y_recv_sem.at[i, j],
-            device_id=(seq_of(lax.rem(my_y + i, y_n), my_z, core), ch), device_id_type=MESH,
-        )
-
-    order = sorted(range(1, z_n), key=lambda i: min(i, z_n - i))
-    for i in order:
-        z_copy(i).start()
-    for j in [0, *order]:
-        if j:
-            z_copy(j).wait_recv()
-        for i in range(1, y_n):
-            y_copy(i, j).start()
-    for j in [0, *order]:
-        for i in range(1, y_n):
-            y_copy(i, j).wait_recv()
-
-    @pl.loop(0, CORES)
-    def _(k):
-        rows = pl.ds(pl.multiple_of(k * rows_dev, rows_dev), rows_dev)
-        stack = table[...].reshape(y_n * z_n * part_rows, LANES)
-        contrib[k] = dot(chosen[rows, :], stack).astype(BF16)
-
-    partner = me + 1 - 2 * core
-    swap = pltpu.make_async_remote_copy(
-        src_ref=contrib.at[1 - core], dst_ref=from_core, send_sem=core_sem.at[0], recv_sem=core_sem.at[1],
-        device_id=(partner, ch), device_id_type=MESH,
-    )
-    swap.start()
-    swap.wait_recv()
-    joined[...] = contrib[core] + from_core[...]
+    def spread(rows, target):
+        for q in range(quads):
+            stage[pl.ds(q, places, quads), :] = rows[:, q * LANES : (q + 1) * LANES]
+        target[...] = stage[: places * quads, :].astype(BF16).reshape(places, quads, LANES)
+
+    spread(total, col_send)
+
+    @pl.loop(1, seq_n)
+    def _(i):
+        peer = seq_peer(i)
+        pltpu.make_async_remote_copy(
+            src_ref=col_send.at[lax.div(peer, CORES)], dst_ref=col_recv.at[me], send_sem=turn_send_sem.at[4],
+            recv_sem=turn_recv_sem.at[4], device_id=(peer, ch), device_id_type=MESH,
+        ).start()
+
+    col_recv[me] = col_send[place]
+    all_in(col_recv, seq_n - 1, 4)
+    column_t = col_recv[...].reshape(blocks, LANES).astype(F32).T.astype(BF16)
+    lane_row = lax.broadcasted_iota(jnp.int32, (LANES, rows_dev), 0).astype(F32)
+
+    @pl.loop(0, places)
+    def _(d):
+        found = dot(column_t, chosen[d])
+        row = side_by_side([map_recv[d, quads + q : quads + q + 1, :] for q in range(quads)])
+        picked = jnp.sum(jnp.where(lane_row == row, found, 0.0), axis=0, keepdims=True)
+        for q in range(quads):
+            stage[pl.ds(d * quads + q, 1), :] = picked[:, q * LANES : (q + 1) * LANES]
+
+    out_send[...] = stage[: places * quads, :].astype(BF16).reshape(places, quads, LANES)
+    out_recv[place] = out_send[place]
+    same_core(lambda peer: out_send.at[peer], lambda: out_recv.at[place], 5)
+    all_in(out_recv, places - 1, 5)
+    stage[: places * quads, :] = out_recv[...].reshape(places * quads, LANES).astype(F32)
+    ordered = side_by_side([stage[pl.ds(q, places, quads), :] for q in range(quads)])
+    joined[ch] = ordered.astype(BF16)
 
     def join_copy(i):
         return pltpu.make_async_remote_copy(
-            src_ref=joined, dst_ref=joined_recv.at[ch], send_sem=join_send_sem.at[i], recv_sem=join_recv_sem.at[i],
+            src_ref=joined.at[ch], dst_ref=joined.at[ch], send_sem=join_send_sem.at[i], recv_sem=join_recv_sem.at[i],
             device_id=(me, ch_peer(i)), device_id_type=MESH,
         )
 
     for i in range(1, ch_n):
-        join_copy(i).start()
-    result = joined[...]
+        go(join_copy(i))
     for i in range(1, ch_n):
         join_copy(i).wait_recv()
-        result = result + joined_recv[lax.rem(ch + ch_n - i, ch_n)]
-    out[...] = result
-
-    swap.wait_send()
-    for i in range(1, ch_n):
-        feature_copy(i).wait_send()
-        term_copy(i).wait_send()
-        emb_copy(i).wait_send()
-        join_copy(i).wait_send()
-    for i in order:
-        z_copy(i).wait_send()
-    for j in [0, *order]:
-        for i in range(1, y_n):
-            y_copy(i, j).wait_send()
+    out[...] = jnp.concatenate([joined[c].astype(F32) for c in range(ch_n)], axis=0).T.astype(BF16)
+
+    for copy in sent:
+        copy.wait_send()
 
 
 def body(sizes, features, w_in, bias_skip, filters, w_out, w_emb, page_lengths, page_owner):
-    seq_n, ch_n, y_n, z_n = sizes
+    seq_n, ch_n = sizes
     rows_dev, chan_dev = features.shape
     width, emb = w_out.shape[0], w_emb.shape[1]
     quads = rows_dev // LANES
     blocks = seq_n * quads
     turn_rows = seq_n * quads * OWNED
-    part_rows = rows_dev // ch_n
-    places = y_n * z_n
+    places = seq_n // CORES
+    share = emb // ch_n
     tables = [jnp.asarray(t) for t in transform_tables(blocks)]
     vmem, sem = pltpu.VMEM, pltpu.SemaphoreType.DMA
     turn = vmem((turn_rows, LANES), BF16)
@@ -430,22 +472,21 @@
         vmem((ch_n, emb, chan_dev), F32),
         vmem((emb, chan_dev), BF16),
         vmem((emb, chan_dev), BF16),
-        vmem((ch_n, part_rows, emb), F32),
-        vmem((ch_n, part_rows, emb), F32),
-        vmem((places, part_rows, emb), BF16),
-        vmem((CORES * rows_dev, places * part_rows), BF16),
-        vmem((CORES, rows_dev, emb), BF16),
-        vmem((rows_dev, emb), BF16),
-        vmem((rows_dev, emb), BF16),
-        vmem((ch_n, rows_dev, emb), BF16),
+        vmem((ch_n, share, rows_dev), F32),
+        vmem((ch_n, share, rows_dev), F32),
+        vmem((2 * quads, LANES), F32),
+        vmem((places, 2 * quads, LANES), F32),
+        vmem((places, blocks, rows_dev), BF16),
+        vmem((places, quads, LANES), BF16),
+        vmem((seq_n, quads, LANES), BF16),
+        vmem((places, quads, LANES), BF16),
+        vmem((places, quads, LANES), BF16),
+        vmem((ch_n, share, rows_dev), BF16),
         sem((10,)),
-        sem((ch_n,)), sem((ch_n,)),
-        sem((3,)), sem((3,)),
+        sem((6,)), sem((6,)),
+        sem((6,)), sem((6,)),
         sem((ch_n,)), sem((ch_n,)),
         sem((ch_n,)), sem((ch_n,)),
-        sem((z_n,)), sem((z_n,)),
-        sem((y_n, z_n)), sem((y_n, z_n)),
-        sem((2,)),
         sem((ch_n,)), sem((ch_n,)),
     ]
     anywhere = pl.BlockSpec(memory_space=pl.ANY)
@@ -474,10 +515,7 @@
 
 
 def solution(mesh):
-    seq_n, ch_n = mesh.shape["seq"], mesh.shape["ch"]
-    places = seq_n // CORES
-    z_n = min(8, max(1, places // 2))
-    sizes = (seq_n, ch_n, places // z_n, z_n)
+    sizes = (mesh.shape["seq"], mesh.shape["ch"])
     return jax.shard_map(
         functools.partial(body, sizes),
         mesh=mesh,

time: 85.7 us -> 76.2 us (0.89)
  Pallas kernels: 84 us -> 74.5 us
    pallas_call x1, Pallas kernels: 84 us -> 74.5 us  [body(): pl.pallas_call(functools.partial(layer_kernel, sizes), out_shape=jax.Shap...]
where the time goes in v2:
time: 76.2 us; the launch traced here: 76.1 us
  Pallas kernels  74.5 us (98%)
  local copies, waits for them, and re-layouts  1.57 us (2%)
    pallas_call x1, Pallas kernels, body(): pl.pallas_call(functools.partial(layer_kernel, sizes), out_shape=jax.Shap...  74.5 us
    unnamed x1, local copies, waits for them, and re-layouts  1.57 us

profile of v2, /device:TPU:1, one launch (start us, length us, event | category | flops | bytes accessed | tf_op | source)
XLA Modules:
  0.0 76.1 jit_solution(6795870943967644498)
XLA Ops:
  0.0 74.5 %hyena_layer.1 = bf16[512,128]{1,0:T(8,128)(2,1)} custom-call(bf16[512,256]{1,0:T(8,128)(2,1)} %features.1, bf16[3,1024,256]{2,1,0:T(8,128)(2,1)} %bitcast.4, f32[1,256]{1,0:T(1,128)} %bitcast.7, f32[512,256]{1,0:T(8,128)} %filters.1, bf16[1024,256]{1,0:T(8,128)(2,1)} %w_out.1, bf16[256,128]{1,0:T(8,128)(2,1)} %w_emb.1, s32[1,512]{1,0:T(1,128)} %bitcast.5, ...), custom_call_target="tpu_custom_call" | custom-call | tf_op jit(solution)/shard_map/hyena_layer/pallas_call | solution.py:494
  74.5 1.6 %copy.15 = bf16[512,128]{1,0:T(8,128)(2,1)} copy(bf16[512,128]{1,0:T(8,128)(2,1)} %hyena_layer.1) | data formatting | bytes 262144

commit v3 on v2

--- a/solution.py
+++ b/solution.py
@@ -103,12 +103,12 @@
     feat, w_vm, w_turned, filt_vm, w_out_vm, w_emb_vm, first_v, twist_v, second_v, second_back_v, last_v,
     stage, filt_send, filt_recv, sig_send, sig_recv, conv_send, conv_recv,
     signal_t, gate_t, spectrum, term_send, term_recv, weight_high, weight_low,
-    emb_send, emb_recv, map_send, map_recv, chosen, col_send, col_recv, out_send, out_recv, joined,
+    emb_send, emb_recv, map_send, map_recv, chosen, col_send, col_recv, out_send, out_recv,
     local_sem, feat_send_sem, feat_recv_sem, turn_send_sem, turn_recv_sem,
     term_send_sem, term_recv_sem, emb_send_sem, emb_recv_sem,
-    join_send_sem, join_recv_sem,
+    heard_sem,
 ):
-    seq_n, ch_n = sizes
+    seq_n, ch_n, y_n, z_n = sizes
     rows_dev, chan_dev = filters.shape
     quads = rows_dev // LANES
     pack = quads * OWNED
@@ -118,6 +118,7 @@
     me, ch = lax.axis_index("seq"), lax.axis_index("ch")
     core = lax.rem(me, CORES)
     place = lax.div(me, CORES)
+    my_y, my_z = lax.div(place, z_n), lax.rem(place, z_n)
 
     def seq_peer(i):
         return lax.rem(me + i, seq_n)
@@ -133,12 +134,19 @@
 
     barrier = pltpu.get_barrier_semaphore()
 
-    @pl.loop(1, seq_n)
-    def _(i):
-        pl.semaphore_signal(barrier, inc=1, device_id=(seq_peer(i), ch), device_id_type=MESH)
-
-    for i in range(1, ch_n):
-        pl.semaphore_signal(barrier, inc=1, device_id=(me, ch_peer(i)), device_id_type=MESH)
+    def seq_of(y, z):
+        return (lax.rem(my_y + y, y_n) * z_n + lax.rem(my_z + z, z_n)) * CORES + core
+
+    partner = me + 1 - 2 * core
+    z_near = sorted({o % z_n for o in (1, 2, -1, -2)} - {0})
+    greeted = [(me, ch_peer(i)) for i in range(1, ch_n)] + [(partner, ch)]
+    greeted += [(seq_of(y, 0), ch) for y in range(1, y_n)] + [(seq_of(0, z), ch) for z in z_near]
+    for device in greeted:
+        pl.semaphore_signal(barrier, inc=1, device_id=device, device_id_type=MESH)
+
+    def tell(n, devices):
+        for device in devices:
+            pl.semaphore_signal(heard_sem.at[n], inc=1, device_id=device, device_id_type=MESH)
 
     loads = [
         (filters, filt_vm), (w_in, w_vm), (features, feat.at[ch]), (first_t, first_v), (twist_t, twist_v),
@@ -203,6 +211,44 @@
         stage[...] = recv[...].astype(F32)
         return side_by_side([stage[pl.ds(c, blocks, OWNED), :] for c in range(OWNED)]).astype(BF16)
 
+    loads[0].wait()
+    chunks_by_channel(filt_vm[...].T, filt_send)
+    pl.semaphore_wait(barrier, len(greeted))
+    loads[2].wait()
+
+    def ring_copy(held, left, right, sems, rows, kind):
+        (lane_of, send_sem, recv_sem) = sems
+        half = rows // 2
+        own, spot, top, device = {
+            "right_low": (1, 1, 0, right), "right_high": (1, 1, 1, right),
+            "left_high": (1, 1, 1, left), "left_low": (1, 1, 0, left),
+            "right_on": (0, 0, 0, right), "left_on": (0, 2, 1, left),
+        }[kind]
+        block = held(spot).at[pl.ds(top * half, half)]
+        n = RING.index(kind)
+        return pltpu.make_async_remote_copy(
+            src_ref=block, dst_ref=block, send_sem=send_sem.at[(*lane_of, n)], recv_sem=recv_sem.at[(*lane_of, n)],
+            device_id=device, device_id_type=MESH,
+        )
+
+    def feature_copy(kind):
+        return ring_copy(
+            lambda spot: feat.at[lax.rem(ch + ch_n - 1 + spot, ch_n)], (me, ch_peer(ch_n - 1)), (me, ch_peer(1)),
+            ((), feat_send_sem, feat_recv_sem), rows_dev, kind,
+        )
+
+    ring_first = RING[:4] if ch_n == 4 else RING[:2]
+    for kind in ring_first:
+        go(feature_copy(kind))
+
+    if z_n == 8:
+        tell(0, [(seq_of(0, 2), ch), (seq_of(0, 6), ch)])
+    loads[1].wait()
+    for b in range(3):
+        w_turned[b] = w_vm[b].T
+    if z_n == 8:
+        pl.semaphore_wait(heard_sem.at[0], 2)
+    tell(1, [(seq_of(y, 0), ch) for y in range(1, y_n)])
     pages = lengths.shape[1]
     length_row = lengths[...].astype(F32)
     owner_row = owners[...].astype(F32)
@@ -232,40 +278,10 @@
         lanes = slice(q * LANES, (q + 1) * LANES)
         map_send[q : q + 1, :] = source_block[:1, lanes]
         map_send[quads + q : quads + q + 1, :] = source_lane[:1, lanes]
-
-    loads[0].wait()
-    chunks_by_channel(filt_vm[...].T, filt_send)
-    loads[1].wait()
-    for b in range(3):
-        w_turned[b] = w_vm[b].T
-
-    pl.semaphore_wait(barrier, seq_n - 1 + ch_n - 1)
-    loads[2].wait()
-
-    def ring_copy(held, left, right, sems, rows, kind):
-        (lane_of, send_sem, recv_sem) = sems
-        half = rows // 2
-        own, spot, top, device = {
-            "right_low": (1, 1, 0, right), "right_high": (1, 1, 1, right),
-            "left_high": (1, 1, 1, left), "left_low": (1, 1, 0, left),
-            "right_on": (0, 0, 0, right), "left_on": (0, 2, 1, left),
-        }[kind]
-        block = held(spot).at[pl.ds(top * half, half)]
-        n = RING.index(kind)
-        return pltpu.make_async_remote_copy(
-            src_ref=block, dst_ref=block, send_sem=send_sem.at[(*lane_of, n)], recv_sem=recv_sem.at[(*lane_of, n)],
-            device_id=device, device_id_type=MESH,
-        )
-
-    def feature_copy(kind):
-        return ring_copy(
-            lambda spot: feat.at[lax.rem(ch + ch_n - 1 + spot, ch_n)], (me, ch_peer(ch_n - 1)), (me, ch_peer(1)),
-            ((), feat_send_sem, feat_recv_sem), rows_dev, kind,
-        )
-
-    ring_first = RING[:4] if ch_n == 4 else RING[:2]
-    for kind in ring_first:
-        go(feature_copy(kind))
+    if y_n > 1:
+        pl.semaphore_wait(heard_sem.at[1], y_n - 1)
+    tell(2, [(partner, ch)])
+    pl.semaphore_wait(heard_sem.at[2], 1)
 
     scatter(filt_send, filt_recv, 0)
     map_recv[place] = map_send[...]
@@ -411,40 +427,40 @@
     column_t = col_recv[...].reshape(blocks, LANES).astype(F32).T.astype(BF16)
     lane_row = lax.broadcasted_iota(jnp.int32, (LANES, rows_dev), 0).astype(F32)
 
-    @pl.loop(0, places)
-    def _(d):
+    def order_rows(d):
         found = dot(column_t, chosen[d])
         row = side_by_side([map_recv[d, quads + q : quads + q + 1, :] for q in range(quads)])
         picked = jnp.sum(jnp.where(lane_row == row, found, 0.0), axis=0, keepdims=True)
-        for q in range(quads):
-            stage[pl.ds(d * quads + q, 1), :] = picked[:, q * LANES : (q + 1) * LANES]
-
-    out_send[...] = stage[: places * quads, :].astype(BF16).reshape(places, quads, LANES)
-    out_recv[place] = out_send[place]
-    same_core(lambda peer: out_send.at[peer], lambda: out_recv.at[place], 5)
-    all_in(out_recv, places - 1, 5)
-    stage[: places * quads, :] = out_recv[...].reshape(places * quads, LANES).astype(F32)
-    ordered = side_by_side([stage[pl.ds(q, places, quads), :] for q in range(quads)])
-    joined[ch] = ordered.astype(BF16)
-
-    def join_copy(i):
-        return pltpu.make_async_remote_copy(
-            src_ref=joined.at[ch], dst_ref=joined.at[ch], send_sem=join_send_sem.at[i], recv_sem=join_recv_sem.at[i],
-            device_id=(me, ch_peer(i)), device_id_type=MESH,
-        )
-
-    for i in range(1, ch_n):
-        go(join_copy(i))
-    for i in range(1, ch_n):
-        join_copy(i).wait_recv()
-    out[...] = jnp.concatenate([joined[c].astype(F32) for c in range(ch_n)], axis=0).T.astype(BF16)
+        lanes = [picked[:, q * LANES : (q + 1) * LANES] for q in range(quads)]
+        out_send[d] = jnp.concatenate(lanes, axis=0).astype(BF16)
+
+    def send_rows(d, first):
+        for i in range(first, ch_n):
+            pltpu.make_async_remote_copy(
+                src_ref=out_send.at[d], dst_ref=out_recv.at[ch * places + place], send_sem=turn_send_sem.at[5],
+                recv_sem=turn_recv_sem.at[5], device_id=(d * CORES + core, ch_peer(i)), device_id_type=MESH,
+            ).start()
+
+    @pl.loop(1, places)
+    def _(i):
+        d = lax.rem(place + i, places)
+        order_rows(d)
+        send_rows(d, 0)
+
+    order_rows(place)
+    send_rows(place, 1)
+    out_recv[ch * places + place] = out_send[place]
+    all_in(out_recv, ch_n * places - 1, 5)
+    rows = ch_n * places
+    stage[: rows * quads, :] = out_recv[...].reshape(rows * quads, LANES).astype(F32)
+    out[...] = side_by_side([stage[pl.ds(q, rows, quads), :] for q in range(quads)]).T.astype(BF16)
 
     for copy in sent:
         copy.wait_send()
 
 
 def body(sizes, features, w_in, bias_skip, filters, w_out, w_emb, page_lengths, page_owner):
-    seq_n, ch_n = sizes
+    seq_n, ch_n, _, _ = sizes
     rows_dev, chan_dev = features.shape
     width, emb = w_out.shape[0], w_emb.shape[1]
     quads = rows_dev // LANES
@@ -480,14 +496,13 @@
         vmem((places, quads, LANES), BF16),
         vmem((seq_n, quads, LANES), BF16),
         vmem((places, quads, LANES), BF16),
-        vmem((places, quads, LANES), BF16),
-        vmem((ch_n, share, rows_dev), BF16),
+        vmem((ch_n * places, quads, LANES), BF16),
         sem((10,)),
         sem((6,)), sem((6,)),
         sem((6,)), sem((6,)),
         sem((ch_n,)), sem((ch_n,)),
         sem((ch_n,)), sem((ch_n,)),
-        sem((ch_n,)), sem((ch_n,)),
+        pltpu.SemaphoreType.REGULAR((3,)),
     ]
     anywhere = pl.BlockSpec(memory_space=pl.ANY)
     inside = pl.BlockSpec(memory_space=pltpu.VMEM)
@@ -514,8 +529,9 @@
     )
 
 
-def solution(mesh):
-    sizes = (mesh.shape["seq"], mesh.shape["ch"])
+def solution(mesh, z_n=8):
+    seq_n, ch_n = mesh.shape["seq"], mesh.shape["ch"]
+    sizes = (seq_n, ch_n, seq_n // CORES // z_n, z_n)
     return jax.shard_map(
         functools.partial(body, sizes),
         mesh=mesh,

time: 76.2 us -> 71.8 us (0.942)
  Pallas kernels: 74.5 us -> 70.1 us
    pallas_call x1, Pallas kernels: 74.5 us -> 70.1 us  [body(): pl.pallas_call(functools.partial(layer_kernel, sizes), out_shape=jax.Shap...]
where the time goes in v3:
time: 71.8 us; the launch traced here: 71.7 us
  Pallas kernels  70.1 us (98%)
  local copies, waits for them, and re-layouts  1.57 us (2%)
    pallas_call x1, Pallas kernels, body(): pl.pallas_call(functools.partial(layer_kernel, sizes), out_shape=jax.Shap...  70.1 us
    unnamed x1, local copies, waits for them, and re-layouts  1.57 us

profile of v3, /device:TPU:1, one launch (start us, length us, event | category | flops | bytes accessed | tf_op | source)
XLA Modules:
  0.0 71.7 jit_solution(314228627018048091)
XLA Ops:
  0.0 70.1 %hyena_layer.1 = bf16[512,128]{1,0:T(8,128)(2,1)} custom-call(bf16[512,256]{1,0:T(8,128)(2,1)} %features.1, bf16[3,1024,256]{2,1,0:T(8,128)(2,1)} %bitcast.4, f32[1,256]{1,0:T(1,128)} %bitcast.7, f32[512,256]{1,0:T(8,128)} %filters.1, bf16[1024,256]{1,0:T(8,128)(2,1)} %w_out.1, bf16[256,128]{1,0:T(8,128)(2,1)} %w_emb.1, s32[1,512]{1,0:T(1,128)} %bitcast.5, ...), custom_call_target="tpu_custom_call" | custom-call | tf_op jit(solution)/shard_map/hyena_layer/pallas_call | solution.py:509
  70.1 1.6 %copy.15 = bf16[512,128]{1,0:T(8,128)(2,1)} copy(bf16[512,128]{1,0:T(8,128)(2,1)} %hyena_layer.1) | data formatting | bytes 262144
